TPU v7x, 32 devices: a whole 2x2x4 slice. The times are simulated.
32 devices in a mesh: grp: 2 (over x), row: 4 (over y, core), col: 4 (over z).
Axes of the slice: x: 2, y: 2, z: 4, core: 2. Of those that a mesh axis runs over, the one named last changes fastest.
Arguments:
- gradients: bfloat16 [2, 3072, 24576], P('grp', 'row', 'col'), may hold values from -6 to 6
- momentum: float32 [2, 3072, 24576], P('grp', 'row', 'col'), may hold values from -94 to 94, as said below
- right_basis: bfloat16 [24576, 512], P('col'), may hold values from -6 to 6
Outputs:
- new_momentum: float32 [2, 3072, 24576], P('grp', 'row', 'col')
- new_basis: bfloat16 [24576, 512], P('col')
- update: bfloat16 [3072, 24576], P('row', 'col')
Inputs may be any that keep to these rules, and one draw needn't show every extreme that they name: Each group's momentum buffer holds real values bounded in magnitude by 94.
All inputs are finite; a program needn't handle non-finite values.
Results may differ from a plain program's by a relative error of at most 0.013.
Values may be sent and summed in bfloat16 or wider, within the bound.
No kernel may reach another device: no remote copies, remote signals or barrier semaphores. Data moves between devices by JAX's collectives and lax.ppermute only.
A program may use at most 192 MiB of HBM per device.

v0:
```python
import math
import jax
import jax.numpy as jnp
from jax import lax
from jax.sharding import PartitionSpec as P

D = 3072
FF = 24576
momentum_decay = 0.9
ridge_scale = 0.0001
epsilon = 1e-06


def per_device(gradients, momentum, right_basis):
    merged = momentum[0] + gradients[0].astype(jnp.float32)
    merged_low = merged.astype(jnp.bfloat16)
    rank = right_basis.shape[1]
    local_rows = merged.shape[0]
    groups = lax.axis_size("grp")
    left_factor = jnp.dot(merged_low, right_basis, preferred_element_type=jnp.float32)
    left_factor = lax.psum(left_factor, ("grp", "col"))
    gram_matrix = jnp.dot(
        left_factor.T,
        left_factor,
        precision=lax.Precision.HIGHEST,
        preferred_element_type=jnp.float32,
    )
    gram_matrix = lax.psum(gram_matrix, "row")
    shifted = gram_matrix + ridge_scale * (jnp.trace(gram_matrix) / rank) * jnp.eye(
        rank, dtype=jnp.float32
    )
    cholesky_factor = jnp.linalg.cholesky(shifted)
    orthonormal = jax.scipy.linalg.solve_triangular(cholesky_factor, left_factor.T, lower=True).T
    orthonormal_low = orthonormal.astype(jnp.bfloat16)
    right_piece = lax.psum_scatter(
        jnp.einsum("ij,ik->jk", merged_low, orthonormal_low, preferred_element_type=jnp.float32)
        / groups,
        ("grp", "row"),
        scatter_dimension=0,
        tiled=True,
    )
    squares_sum = lax.psum(jnp.sum(right_piece * right_piece, axis=0), ("grp", "row", "col"))
    column_rms = jnp.sqrt(squares_sum / FF + epsilon)
    basis_piece = (right_piece / column_rms).astype(jnp.bfloat16)
    new_basis = lax.all_gather(basis_piece, ("grp", "row"), axis=0, tiled=True)
    scaled_low = (orthonormal * column_rms).astype(jnp.bfloat16)
    stacked_left = jnp.concatenate([orthonormal_low, scaled_low], axis=0)
    products = lax.dot_general(
        stacked_left, new_basis, (((1,), (1,)), ((), ())), preferred_element_type=jnp.float32
    )
    update = (math.sqrt(D / rank) * products[:local_rows]).astype(jnp.bfloat16)
    new_momentum = merged - (1 - momentum_decay) * products[local_rows:]
    return (new_momentum[None], new_basis, update)


def solution(mesh):
    placed = (P("grp", "row", "col"), P("grp", "row", "col"), P("col", None))
    return jax.shard_map(
        per_device,
        mesh=mesh,
        in_specs=placed,
        out_specs=(P("grp", "row", "col"), P("col", None), P("row", "col")),
        check_vma=False,
    )
```

profile of v0, /device:TPU:0, one launch (start us, length us, event | category | flops | bytes accessed | tf_op | source)
XLA Modules:
  0.0 571.5 jit_solution(11298034672186041902)
XLA Ops:
  7.2 14.6 %fusion.42 = f32[768,512]{1,0:T(8,128)} fusion(bf16[6144,512]{1,0:T(8,128)(2,1)} %param.5, f32[1,768,6144]{2,1,0:T(8,128)} %param.4, bf16[1,768,6144]{2,1,0:T(8,128)(2,1)} %param.3), kind=kOutput, calls=%fused_computation.89 | convolution fusion | flops 4845993984 | bytes 36175872 | tf_op jit(solution)/shard_map/dot_general | solution.py:20
  21.9 92.1 %all-reduce.4.cloned.1.call-done = f32[768,512]{1,0:T(8,128)} async-done(((f32[768,512]{1,0:T(8,128)}), f32[768,512]{1,0:T(8,128)}) %all-reduce.4.cloned.1.call-update) | async-done | bytes 1572880 | tf_op jit(solution)/shard_map/psum | solution.py:21
  114.0 5.6 fusion.44
  119.9 35.5 %all-reduce.6.cloned.1.call-done = f32[512,512]{0,1:T(8,128)} async-done(((f32[512,512]{0,1:T(8,128)}), f32[512,512]{0,1:T(8,128)}) %all-reduce.6.cloned.1.call-update) | async-done | bytes 1048592 | tf_op jit(solution)/shard_map/psum | solution.py:28
  155.3 2.0 select_reduce_fusion
  158.7 11.7 %cholesky.103 = f32[128,128]{1,0:T(8,128)S(1)} custom-call(f32[128,128]{1,0:T(8,128)S(1)} %cholesky.263), custom_call_target="Cholesky" | custom-call | tf_op jit(solution)/shard_map/jit(cholesky)/cholesky | solution.py:32
  170.6 9.8 %custom-call.31 = f32[1,128,128]{1,2,0:T(8,128)S(1)} custom-call(f32[1,128,128]{2,1,0:T(8,128)S(1)} %get-tuple-element.32), custom_call_target="InvertDiagBlocksLowerTriangular" | custom-call | tf_op jit(solution)/shard_map/jit(cholesky)/cholesky | solution.py:32
  181.2 11.7 %cholesky.215 = f32[128,128]{1,0:T(8,128)S(1)} custom-call(f32[128,128]{1,0:T(8,128)S(1)} %cholesky.267), custom_call_target="Cholesky" | custom-call | tf_op jit(solution)/shard_map/jit(cholesky)/cholesky | solution.py:32
  193.0 10.0 %custom-call.32 = f32[1,128,128]{1,2,0:T(8,128)S(1)} custom-call(f32[1,128,128]{2,1,0:T(8,128)S(1)} %get-tuple-element.30), custom_call_target="InvertDiagBlocksLowerTriangular" | custom-call | tf_op jit(solution)/shard_map/jit(cholesky)/cholesky | solution.py:32
  203.5 0.6 convolution_subtract_fusion.4
  204.1 11.7 %cholesky.236 = f32[128,128]{1,0:T(8,128)S(1)} custom-call(f32[128,128]{1,0:T(8,128)S(1)} %cholesky.272), custom_call_target="Cholesky" | custom-call | tf_op jit(solution)/shard_map/jit(cholesky)/cholesky | solution.py:32
  216.0 9.8 %custom-call.33 = f32[1,128,128]{1,2,0:T(8,128)S(1)} custom-call(f32[1,128,128]{2,1,0:T(8,128)S(1)} %get-tuple-element.28), custom_call_target="InvertDiagBlocksLowerTriangular" | custom-call | tf_op jit(solution)/shard_map/jit(cholesky)/cholesky | solution.py:32
  226.6 12.1 %cholesky.253 = f32[128,128]{1,0:T(8,128)S(1)} custom-call(f32[128,128]{1,0:T(8,128)S(1)} %convolution_subtract_fusion.5), custom_call_target="Cholesky" | custom-call | tf_op jit(solution)/shard_map/jit(cholesky)/cholesky | solution.py:32
  238.8 0.7 compare_reduce_fusion.1
  239.5 0.7 compare_reduce_fusion
  240.2 0.7 compare_reduce_fusion.2
  243.4 1.1 select_select_fusion
  244.5 14.5 %while.1 = (s32[]{:T(128)}, f32[512,512]{0,1:T(8,128)}, s32[4,2]{0,1:T(2,128)S(1)}, f32[4,128,128]{2,1,0:T(8,128)}, s32[]{:T(128)}) while((s32[]{:T(128)}, f32[512,512]{0,1:T(8,128)}, s32[4,2]{0,1:T(2,128)S(1)}, f32[4,128,128]{2,1,0:T(8,128)}, s32[]{:T(128)}) %tuple.29), condition=%wide.while_cond, body=%wide.while_body.sunk | while | flops 2 | bytes 393329 | solution.py:33
  244.6 0.6 fusion.55
  245.2 2.2 dynamic-slice.7
  247.5 0.6 bitcast_dynamic-update-slice_fusion.2
  248.2 0.6 fusion.55
  248.8 2.2 dynamic-slice.7
  251.2 0.6 bitcast_dynamic-update-slice_fusion.2
  251.9 0.6 fusion.55
  252.5 2.2 dynamic-slice.7
  254.8 0.6 bitcast_dynamic-update-slice_fusion.2
  255.5 0.6 fusion.55
  256.1 2.2 dynamic-slice.7
  258.4 0.6 bitcast_dynamic-update-slice_fusion.2
  259.0 40.1 %custom-call.34 = f32[4,128,128]{1,2,0:T(8,128)S(1)} custom-call(f32[4,128,128]{2,1,0:T(8,128)} %get-tuple-element.10), custom_call_target="InvertDiagBlocksLowerTriangular" | custom-call | tf_op jit(solution)/shard_map/jit(_solve_triangular)/triangular_solve | solution.py:33
  299.1 0.5 fusion.18
  299.7 1.6 convolution_subtract_fusion.1
  301.3 0.5 fusion.31
  301.8 2.3 convolution_subtract_fusion.2
  304.2 0.5 fusion.29
  304.7 3.0 convolution_subtract_fusion
  307.7 0.5 fusion.28
  308.2 19.8 %convolution_multiply_fusion = f32[6144,512]{1,0:T(8,128)} fusion(f32[128,768]{1,0:T(8,128)S(1)} %fusion.28, f32[128,768]{1,0:T(8,128)S(1)} %fusion.29, f32[128,768]{1,0:T(8,128)S(1)} %fusion.31, f32[128,768]{1,0:T(8,128)S(1)} %fusion.18, f32[1,768,6144]{2,1,0:T(8,128)} %param.4, bf16[1,768,6144]{2,1,0:T(8,128)(2,1)} %param.3), kind=kOutput, calls=%fused_computation.9 | convolution fusion | flops 4852285440 | bytes 42467328 | tf_op jit(solution)/shard_map/ij,ik->jk/dot_general | solution.py:36
  328.1 92.8 %reduce-scatter.2.cloned.1.call-done = f32[768,512]{1,0:T(8,128)} async-done(((f32[6144,512]{1,0:T(8,128)}), f32[768,512]{1,0:T(8,128)}) %reduce-scatter.2.cloned.1.call-update) | async-done | bytes 1572880 | tf_op jit(solution)/shard_map/reduce_scatter | solution.py:35
  420.9 1.6 multiply_reduce_fusion
  422.5 39.3 %psum.23 = f32[512]{0:T(512)S(1)} all-reduce(f32[512]{0:T(512)S(1)} %multiply_reduce_fusion), channel_id=1, replica_groups=mesh['grp'=2,'row'=4,'col'=4] {'grp','row','col'}, use_global_device_ids=true, to_apply=%region_13.14 | all-reduce | flops 512 | bytes 4096 | tf_op jit(solution)/shard_map/psum | solution.py:42
  461.8 2.5 divide_convert_fusion
  464.4 1.0 fusion.14
  465.4 45.2 %all-gather.2.cloned.1.call-done = bf16[6144,512]{1,0:T(8,128)(2,1)} async-done(((bf16[768,512]{1,0:T(8,128)(2,1)}), bf16[6144,512]{1,0:T(8,128)(2,1)}) %all-gather.2.cloned.1.call-update) | async-done | bytes 6291472 | tf_op jit(solution)/shard_map/all_gather | solution.py:45
  510.6 19.5 %fusion.3 = f32[1536,6144]{1,0:T(8,128)} fusion(bf16[6144,512]{1,0:T(8,128)(2,1)} %all-gather.2.cloned.1.call-done, bf16[768,512]{0,1:T(8,128)(2,1)} %fusion.14, bf16[768,512]{0,1:T(8,128)(2,1)S(1)} %fusion.41), kind=kOutput, calls=%fused_computation.11 | convolution fusion | flops 9666822144 | bytes 45613056 | tf_op jit(solution)/shard_map/dot_general | solution.py:48
  530.1 32.0 %fusion = (bf16[768,6144]{1,0:T(8,128)(2,1)}, f32[1,768,6144]{2,1,0:T(8,128)}) fusion(f32[1536,6144]{1,0:T(8,128)} %fusion.3, f32[1,768,6144]{2,1,0:T(8,128)} %param.4, bf16[1,768,6144]{2,1,0:T(8,128)(2,1)} %param.3), kind=kLoop, calls=%fused_computation.3 | loop fusion | flops 28311552 | bytes 94371840 | tf_op jit(solution)/shard_map/convert_element_type | solution.py:51
  562.1 2.7 copy.40
  (55 shorter events, 4.4 us)
Async XLA Ops:
  7.2 106.9 %all-reduce.4.cloned.1.call-start = ((), (), s32[]{:S(2)}) async-start(), calls=%async_computation.1 | async-start | bytes 3145728 | tf_op jit(solution)/shard_map/psum | solution.py:21
  21.9 133.5 %all-reduce.6.cloned.1.call-start = ((), (), s32[]{:S(2)}) async-start(), calls=%async_computation.2 | async-start | bytes 2097152 | tf_op jit(solution)/shard_map/psum | solution.py:28
  119.6 301.3 %reduce-scatter.2.cloned.1.call-start = ((), (), s32[]{:S(2)}) async-start(), calls=%async_computation.3 | async-start | bytes 14155776 | tf_op jit(solution)/shard_map/reduce_scatter | solution.py:35
  155.3 2.6 copy-start.1
  243.4 55.7 %copy-start = (f32[768,512]{1,0:T(8,128)S(1)}, f32[768,512]{1,0:T(8,128)}, u32[]{:S(2)}) copy-start(f32[768,512]{1,0:T(8,128)} %all-reduce.4.cloned.1.call-done) | copy-start | bytes 4718596
  328.0 182.6 %all-gather.2.cloned.1.call-start = ((), (), s32[]{:S(2)}) async-start(), calls=%async_computation.4 | async-start | bytes 7077888 | tf_op jit(solution)/shard_map/all_gather | solution.py:45
  510.6 51.4 %slice-start = ((s8[6291456]{0:T(1024)(128)(4,1)}), s8[2097152]{0:T(1024)(128)(4,1)S(1)}, s32[]{:S(2)}) async-start(s8[6291456]{0:T(1024)(128)(4,1)} %bitcast.66), calls=%async_computation.5 | async-start | bytes 4194304
  530.1 32.0 %slice-start.1 = ((s8[6291456]{0:T(1024)(128)(4,1)}), s8[4194304]{0:T(1024)(128)(4,1)S(1)}, s32[]{:S(2)}) async-start(s8[6291456]{0:T(1024)(128)(4,1)} %bitcast.66), calls=%async_computation.6 | async-start | bytes 8388608
Sparse Core Ops, SparseCore 0:
  22.0 92.0 all-reduce.3
  119.7 35.5 all-reduce.5
  328.2 92.7 reduce-scatter.1
  464.4 46.1 all-gather.1
where the time goes:
time: 576 us; the launch traced here: 571 us
  waiting for transfers between devices  266 us (46%)
  other arithmetic  160 us (28%)
  matrix products  70.8 us (12%)
  blocking collectives  39.3 us (7%)
  local copies, waits for them, and re-layouts  18.2 us (3%)
  between operations  17.4 us (3%)
    reduce_scatter x1, waiting for transfers between devices, per_device(): lax.psum_scatter(jnp.einsum('ij,ik->jk', merged_low, orthonormal_low, pre...  92.8 us
    psum x1, waiting for transfers between devices, per_device(): left_factor = lax.psum(left_factor, ('grp', 'col'))  92.1 us
    another operation x14, other arithmetic, per_device(): cholesky_factor = jnp.linalg.cholesky(shifted)  79 us
    all_gather x1, waiting for transfers between devices, per_device(): new_basis = lax.all_gather(basis_piece, ('grp', 'row'), axis=0, tiled=True)  45.2 us
    another operation x3, other arithmetic, per_device(): jax.scipy.linalg.solve_triangular(cholesky_factor, left_factor.T, lower=T...  41.2 us
    psum x1, blocking collectives, per_device(): lax.psum(jnp.sum(right_piece * right_piece, axis=0), ('grp', 'row', 'col'))  39.3 us
    psum x1, waiting for transfers between devices, per_device(): gram_matrix = lax.psum(gram_matrix, 'row')  35.5 us
    convert_element_type x1, other arithmetic, per_device(): update = (math.sqrt(D / rank) * products[:local_rows]).astype(jnp.bfloat16)  32 us
  transfers between devices with their start and end apart: 4, of which 4 were waited for; matrix products, arithmetic and copies ran while one was open for 0% of the time, Pallas kernels for 0%

commit v1 on v0

--- a/solution.py
+++ b/solution.py
@@ -18,7 +18,7 @@
     local_rows = merged.shape[0]
     groups = lax.axis_size("grp")
     left_factor = jnp.dot(merged_low, right_basis, preferred_element_type=jnp.float32)
-    left_factor = lax.psum(left_factor, ("grp", "col"))
+    left_factor = jnp.sum(lax.all_gather(left_factor, ("grp", "col")), axis=0)
     gram_matrix = jnp.dot(
         left_factor.T,
         left_factor,

time: 576 us -> 675 us (1.17)
  waiting for transfers between devices: 266 us -> 351 us
  other arithmetic: 160 us -> 169 us
    all_gather x0 -> x1, waiting for transfers between devices: none -> 179 us  [per_device(): left_factor = jnp.sum(lax.all_gather(left_factor, ('grp', 'col')), axis=0)]
    psum x1 -> x0, waiting for transfers between devices: 92.1 us -> none  [per_device(): left_factor = lax.psum(left_factor, ('grp', 'col'))]
where the time goes in v1:
time: 675 us; the launch traced here: 669 us
  waiting for transfers between devices  351 us (52%)
  other arithmetic  169 us (25%)
  matrix products  72.5 us (11%)
  blocking collectives  39.3 us (6%)
  local copies, waits for them, and re-layouts  19.2 us (3%)
  between operations  17.4 us (3%)
    all_gather x1, waiting for transfers between devices, per_device(): left_factor = jnp.sum(lax.all_gather(left_factor, ('grp', 'col')), axis=0)  179 us
    reduce_scatter x1, waiting for transfers between devices, per_device(): lax.psum_scatter(jnp.einsum('ij,ik->jk', merged_low, orthonormal_low, pre...  92.8 us
    another operation x14, other arithmetic, per_device(): cholesky_factor = jnp.linalg.cholesky(shifted)  79 us
    all_gather x1, waiting for transfers between devices, per_device(): new_basis = lax.all_gather(basis_piece, ('grp', 'row'), axis=0, tiled=True)  45.2 us
    another operation x3, other arithmetic, per_device(): jax.scipy.linalg.solve_triangular(cholesky_factor, left_factor.T, lower=T...  40.4 us
    psum x1, blocking collectives, per_device(): lax.psum(jnp.sum(right_piece * right_piece, axis=0), ('grp', 'row', 'col'))  39.3 us
    psum x1, waiting for transfers between devices, per_device(): gram_matrix = lax.psum(gram_matrix, 'row')  34.4 us
    convert_element_type x1, other arithmetic, per_device(): update = (math.sqrt(D / rank) * products[:local_rows]).astype(jnp.bfloat16)  32 us
  transfers between devices with their start and end apart: 4, of which 4 were waited for; matrix products, arithmetic and copies ran while one was open for 0% of the time, Pallas kernels for 0%

profile of v1, /device:TPU:0, one launch (start us, length us, event | category | flops | bytes accessed | tf_op | source)
XLA Modules:
  0.0 669.0 jit_solution(4554695794556082581)
XLA Ops:
  7.2 14.6 %fusion.42 = f32[768,512]{1,0:T(8,128)} fusion(bf16[6144,512]{1,0:T(8,128)(2,1)} %param.5, f32[1,768,6144]{2,1,0:T(8,128)} %param.4, bf16[1,768,6144]{2,1,0:T(8,128)(2,1)} %param.3), kind=kOutput, calls=%fused_computation.89 | convolution fusion | flops 4845993984 | bytes 36175872 | tf_op jit(solution)/shard_map/dot_general | solution.py:20
  21.9 178.9 %all-gather.6.cloned.1.call-done = f32[6144,512]{1,0:T(8,128)} async-done(((f32[768,512]{1,0:T(8,128)}), f32[6144,512]{1,0:T(8,128)}) %all-gather.6.cloned.1.call-update) | async-done | bytes 12582928 | tf_op jit(solution)/shard_map/all_gather | solution.py:21
  200.8 6.3 reduce_sum.28
  207.2 3.7 fusion.44
  211.1 34.4 %all-reduce.3.cloned.1.call-done = f32[512,512]{0,1:T(8,128)} async-done(((f32[512,512]{0,1:T(8,128)}), f32[512,512]{0,1:T(8,128)}) %all-reduce.3.cloned.1.call-update) | async-done | bytes 1048592 | tf_op jit(solution)/shard_map/psum | solution.py:28
  245.5 2.0 select_reduce_fusion
  248.1 2.3 select_add_fusion
  250.5 2.5 copy.7
  253.0 1.4 fusion.12
  254.5 1.0 copy-done.1
  255.4 11.7 %cholesky.103 = f32[128,128]{1,0:T(8,128)S(1)} custom-call(f32[128,128]{1,0:T(8,128)S(1)} %cholesky.263), custom_call_target="Cholesky" | custom-call | tf_op jit(solution)/shard_map/jit(cholesky)/cholesky | solution.py:32
  267.3 9.8 %custom-call.31 = f32[1,128,128]{1,2,0:T(8,128)S(1)} custom-call(f32[1,128,128]{2,1,0:T(8,128)S(1)} %get-tuple-element.32), custom_call_target="InvertDiagBlocksLowerTriangular" | custom-call | tf_op jit(solution)/shard_map/jit(cholesky)/cholesky | solution.py:32
  277.1 1.2 fusion.23
  278.3 1.3 convolution_subtract_fusion.3
  279.8 11.7 %cholesky.215 = f32[128,128]{1,0:T(8,128)S(1)} custom-call(f32[128,128]{1,0:T(8,128)S(1)} %cholesky.267), custom_call_target="Cholesky" | custom-call | tf_op jit(solution)/shard_map/jit(cholesky)/cholesky | solution.py:32
  291.6 10.0 %custom-call.32 = f32[1,128,128]{1,2,0:T(8,128)S(1)} custom-call(f32[1,128,128]{2,1,0:T(8,128)S(1)} %get-tuple-element.30), custom_call_target="InvertDiagBlocksLowerTriangular" | custom-call | tf_op jit(solution)/shard_map/jit(cholesky)/cholesky | solution.py:32
  302.1 1.5 convolution_subtract_fusion.4
  303.6 11.7 %cholesky.236 = f32[128,128]{1,0:T(8,128)S(1)} custom-call(f32[128,128]{1,0:T(8,128)S(1)} %cholesky.272), custom_call_target="Cholesky" | custom-call | tf_op jit(solution)/shard_map/jit(cholesky)/cholesky | solution.py:32
  315.5 9.8 %custom-call.33 = f32[1,128,128]{1,2,0:T(8,128)S(1)} custom-call(f32[1,128,128]{2,1,0:T(8,128)S(1)} %get-tuple-element.28), custom_call_target="InvertDiagBlocksLowerTriangular" | custom-call | tf_op jit(solution)/shard_map/jit(cholesky)/cholesky | solution.py:32
  325.6 1.3 convolution_subtract_fusion.5
  326.9 12.1 %cholesky.253 = f32[128,128]{1,0:T(8,128)S(1)} custom-call(f32[128,128]{1,0:T(8,128)S(1)} %convolution_subtract_fusion.5), custom_call_target="Cholesky" | custom-call | tf_op jit(solution)/shard_map/jit(cholesky)/cholesky | solution.py:32
  339.2 0.7 compare_reduce_fusion.1
  339.9 0.6 compare_reduce_fusion
  340.5 0.6 compare_reduce_fusion.2
  343.7 1.1 select_select_fusion
  344.8 12.5 %while.1 = (s32[]{:T(128)}, f32[512,512]{0,1:T(8,128)}, s32[4,2]{0,1:T(2,128)S(1)}, f32[4,128,128]{2,1,0:T(8,128)S(1)}, s32[]{:T(128)}) while((s32[]{:T(128)}, f32[512,512]{0,1:T(8,128)}, s32[4,2]{0,1:T(2,128)S(1)}, f32[4,128,128]{2,1,0:T(8,128)S(1)}, s32[]{:T(128)}) %tuple.29), condition=%wide.while_cond, body=%wide.while_body.sunk | while | flops 2 | bytes 393329 | solution.py:33
  344.9 0.6 fusion.55
  345.5 2.3 dynamic-slice.7
  348.0 0.6 fusion.55
  348.6 2.3 dynamic-slice.7
  351.2 0.6 fusion.55
  351.8 2.3 dynamic-slice.7
  354.3 0.6 fusion.55
  354.9 2.3 dynamic-slice.7
  357.3 39.3 %custom-call.34 = f32[4,128,128]{1,2,0:T(8,128)S(1)} custom-call(f32[4,128,128]{2,1,0:T(8,128)S(1)} %get-tuple-element.10), custom_call_target="InvertDiagBlocksLowerTriangular" | custom-call | tf_op jit(solution)/shard_map/jit(_solve_triangular)/triangular_solve | solution.py:33
  397.2 1.6 convolution_subtract_fusion.1
  399.3 2.3 convolution_subtract_fusion.2
  402.2 3.0 convolution_subtract_fusion
  405.7 19.8 %convolution_multiply_fusion = f32[6144,512]{1,0:T(8,128)} fusion(f32[128,768]{1,0:T(8,128)S(1)} %fusion.28, f32[128,768]{1,0:T(8,128)S(1)} %fusion.29, f32[128,768]{1,0:T(8,128)S(1)} %fusion.31, f32[128,768]{1,0:T(8,128)S(1)} %fusion.18, f32[1,768,6144]{2,1,0:T(8,128)} %param.4, bf16[1,768,6144]{2,1,0:T(8,128)(2,1)} %param.3), kind=kOutput, calls=%fused_computation.9 | convolution fusion | flops 4852285440 | bytes 42467328 | tf_op jit(solution)/shard_map/ij,ik->jk/dot_general | solution.py:36
  425.6 92.8 %reduce-scatter.2.cloned.1.call-done = f32[768,512]{1,0:T(8,128)} async-done(((f32[6144,512]{1,0:T(8,128)}), f32[768,512]{1,0:T(8,128)}) %reduce-scatter.2.cloned.1.call-update) | async-done | bytes 1572880 | tf_op jit(solution)/shard_map/reduce_scatter | solution.py:35
  518.4 1.6 multiply_reduce_fusion
  520.0 39.3 %psum.15 = f32[512]{0:T(512)S(1)} all-reduce(f32[512]{0:T(512)S(1)} %multiply_reduce_fusion), channel_id=1, replica_groups=mesh['grp'=2,'row'=4,'col'=4] {'grp','row','col'}, use_global_device_ids=true, to_apply=%region_13.14 | all-reduce | flops 512 | bytes 4096 | tf_op jit(solution)/shard_map/psum | solution.py:42
  559.3 2.5 divide_convert_fusion
  561.9 1.0 fusion.14
  562.9 45.2 %all-gather.4.cloned.1.call-done = bf16[6144,512]{1,0:T(8,128)(2,1)} async-done(((bf16[768,512]{1,0:T(8,128)(2,1)}), bf16[6144,512]{1,0:T(8,128)(2,1)}) %all-gather.4.cloned.1.call-update) | async-done | bytes 6291472 | tf_op jit(solution)/shard_map/all_gather | solution.py:45
  608.1 19.5 %fusion.3 = f32[1536,6144]{1,0:T(8,128)} fusion(bf16[6144,512]{1,0:T(8,128)(2,1)} %all-gather.4.cloned.1.call-done, bf16[768,512]{0,1:T(8,128)(2,1)} %fusion.14, bf16[768,512]{0,1:T(8,128)(2,1)S(1)} %fusion.41), kind=kOutput, calls=%fused_computation.11 | convolution fusion | flops 9666822144 | bytes 45613056 | tf_op jit(solution)/shard_map/dot_general | solution.py:48
  627.6 32.0 %fusion = (bf16[768,6144]{1,0:T(8,128)(2,1)}, f32[1,768,6144]{2,1,0:T(8,128)}) fusion(f32[1536,6144]{1,0:T(8,128)} %fusion.3, f32[1,768,6144]{2,1,0:T(8,128)} %param.4, bf16[1,768,6144]{2,1,0:T(8,128)(2,1)} %param.3), kind=kLoop, calls=%fused_computation.3 | loop fusion | flops 28311552 | bytes 94371840 | tf_op jit(solution)/shard_map/convert_element_type | solution.py:51
  659.6 2.7 copy.39
  (56 shorter events, 4.7 us)
Async XLA Ops:
  7.2 193.7 %all-gather.6.cloned.1.call-start = ((), (), s32[]{:S(2)}) async-start(), calls=%async_computation.4 | async-start | bytes 14155776 | tf_op jit(solution)/shard_map/all_gather | solution.py:21
  21.9 223.7 %all-reduce.3.cloned.1.call-start = ((), (), s32[]{:S(2)}) async-start(), calls=%async_computation.1 | async-start | bytes 2097152 | tf_op jit(solution)/shard_map/psum | solution.py:28
  210.9 307.5 %reduce-scatter.2.cloned.1.call-start = ((), (), s32[]{:S(2)}) async-start(), calls=%async_computation.2 | async-start | bytes 14155776 | tf_op jit(solution)/shard_map/reduce_scatter | solution.py:35
  245.5 7.5 %copy-start = (f32[512,512]{0,1:T(8,128)S(1)}, f32[512,512]{0,1:T(8,128)}, u32[]{:S(2)}) copy-start(f32[512,512]{0,1:T(8,128)} %all-reduce.3.cloned.1.call-done) | copy-start | bytes 3145732
  254.4 1.0 copy-start.1
  425.5 182.6 %all-gather.4.cloned.1.call-start = ((), (), s32[]{:S(2)}) async-start(), calls=%async_computation.3 | async-start | bytes 7077888 | tf_op jit(solution)/shard_map/all_gather | solution.py:45
  608.1 51.4 %slice-start = ((s8[6291456]{0:T(1024)(128)(4,1)}), s8[2097152]{0:T(1024)(128)(4,1)S(1)}, s32[]{:S(2)}) async-start(s8[6291456]{0:T(1024)(128)(4,1)} %bitcast.68), calls=%async_computation.5 | async-start | bytes 4194304
  627.6 32.0 %slice-start.1 = ((s8[6291456]{0:T(1024)(128)(4,1)}), s8[4194304]{0:T(1024)(128)(4,1)S(1)}, s32[]{:S(2)}) async-start(s8[6291456]{0:T(1024)(128)(4,1)} %bitcast.68), calls=%async_computation.6 | async-start | bytes 8388608
Sparse Core Ops, SparseCore 0:
  22.0 178.8 all-gather.5
  211.0 34.4 all-reduce.2
  425.6 92.7 reduce-scatter.1
  561.9 46.1 all-gather.3
